TPU v7x, 32 devices: a whole 2x2x4 slice. The times are simulated.
32 devices in a mesh: dp: 8 (over z, x), seq: 4 (over y, core).
Axes of the slice: x: 2, y: 2, z: 4, core: 2. Of those that a mesh axis runs over, the one named last changes fastest.
Arguments:
- tokens: bfloat16 [8, 1024, 1600], P('dp', 'seq'), may hold values from -6 to 6
- cotangent: bfloat16 [8, 1024, 1600], P('dp', 'seq'), may hold values from -6 to 6
- lengths: int32 [8], P('dp'), may hold values from 256 to 1024, as said below
- w_qkv: bfloat16 [7680000], P(('dp', 'seq')), may hold values from -0.15625 to 0.15625
- w_out: bfloat16 [2560000], P(('dp', 'seq')), may hold values from -2.5 to 2.5
- w_fc: bfloat16 [10246400], P(('dp', 'seq')), may hold values from -0.15625 to 0.15625
- w_proj: bfloat16 [10240000], P(('dp', 'seq')), may hold values from -0.078125 to 0.078125
- attention_vectors: bfloat16 [6400], P(('dp', 'seq')), as said below
- block_vectors: bfloat16 [6400], P(('dp', 'seq')), as said below
Outputs:
- output: bfloat16 [8, 1024, 1600], P('dp', 'seq')
- input_grad: float32 [8, 1024, 1600], P('dp', 'seq')
- grad_qkv: float32 [7680000], P(('dp', 'seq'))
- grad_out: float32 [2560000], P(('dp', 'seq'))
- grad_fc: float32 [10246400], P(('dp', 'seq'))
- grad_proj: float32 [10240000], P(('dp', 'seq'))
- grad_attention_vectors: float32 [6400], P(('dp', 'seq'))
- grad_block_vectors: float32 [6400], P(('dp', 'seq'))
Inputs may be any that keep to these rules, and one draw needn't show every extreme that they name: `lengths`: valid positions of each slot; in every draw one slot has all 1024 and one has 256. `attention_vectors`: gains near one, biases of order one half. `block_vectors`: gains near one, biases of order one half.
All inputs are finite; a program needn't handle non-finite values.
Results may differ from a plain program's by a relative error of at most 0.01.
Values may be sent and summed in bfloat16 or wider, within the bound.
No kernel may reach another device: no remote copies, remote signals or barrier semaphores. Data moves between devices by JAX's collectives and lax.ppermute only.
A program may use at most 448 MiB of HBM per device.

v0:
```python
from functools import partial
import jax
import jax.numpy as jnp
from jax import lax
from jax.sharding import PartitionSpec as P

HD = 64
EPS = 1e-05


def layer_norm(value, gain, shift):
    centre = value - jnp.mean(value, axis=-1, keepdims=True)
    spread = jnp.mean(centre * centre, axis=-1, keepdims=True)
    return centre * lax.rsqrt(spread + EPS) * gain + shift


def tanh_gelu(value):
    return jax.nn.gelu(value, approximate=True)


def split_weights(gathered, width):
    flat_qkv, flat_out, flat_fc, flat_proj, first_vectors, second_vectors = gathered
    hidden = flat_fc.shape[0] // (width + 1)
    expand_full = flat_fc.reshape(width + 1, hidden)
    token_rows = (
        jnp.concatenate([first_vectors, second_vectors]).astype(jnp.float32).reshape(8, width)
    )
    expand_bias = expand_full[width].astype(jnp.float32)
    return (
        flat_qkv.reshape(width, 3 * width),
        flat_out.reshape(width, width),
        expand_full[:width],
        flat_proj.reshape(hidden, width),
        token_rows,
        expand_bias,
    )


def to_heads(value, heads):
    slots, count, width = value.shape
    return jnp.moveaxis(value.reshape(slots, count, heads, width // heads), 2, 0)


def from_heads(value):
    heads, slots, count, size = value.shape
    return jnp.moveaxis(value, 0, 2).reshape(slots, count, heads * size)


def head_scores(allowed, query, keys):
    scores = jnp.einsum("sqd,skd->sqk", query, keys, preferred_element_type=jnp.float32) * 0.125
    return jnp.where(allowed, scores, -1e30)


def head_forward(allowed, item):
    query, keys, values = item
    scores = head_scores(allowed, query, keys)
    peak = jnp.max(scores, axis=-1, keepdims=True)
    raised = jnp.exp(scores - peak)
    total = jnp.sum(raised, axis=-1, keepdims=True)
    weights = (raised / total).astype(jnp.bfloat16)
    result = jnp.einsum("sqk,skd->sqd", weights, values, preferred_element_type=jnp.float32)
    return (result, (peak + jnp.log(total))[..., 0])


def head_backward(allowed, item):
    query, keys, values, grad_result, normal = item
    scores = head_scores(allowed, query, keys)
    probs = jnp.where(allowed, jnp.exp(scores - normal[..., None]), 0.0)
    weights = probs.astype(jnp.bfloat16)
    grad_probs = jnp.einsum("sqd,skd->sqk", grad_result, values, preferred_element_type=jnp.float32)
    inner_total = jnp.sum(probs * grad_probs, axis=-1, keepdims=True)
    grad_scores = (probs * (grad_probs - inner_total) * 0.125).astype(jnp.bfloat16)
    grad_query = jnp.einsum("sqk,skd->sqd", grad_scores, keys, preferred_element_type=jnp.float32)
    grad_keys = jnp.einsum("sqk,sqd->skd", grad_scores, query, preferred_element_type=jnp.float32)
    grad_values = jnp.einsum(
        "sqk,sqd->skd", weights, grad_result, preferred_element_type=jnp.float32
    )
    return (grad_query, grad_keys, grad_values)


def local(tokens, cotangent, lengths, w_qkv, w_out, w_fc, w_proj, attention_vectors, block_vectors):
    slots, count, width = tokens.shape
    heads = width // HD
    rank = lax.axis_index("seq")
    span = count * lax.axis_size("seq")
    part_qkv, part_out, part_fc, part_proj, part_first, part_second = (
        lax.all_gather(w_qkv, "seq", axis=0, tiled=True),
        lax.all_gather(w_out, "seq", axis=0, tiled=True),
        lax.all_gather(w_fc, "seq", axis=0, tiled=True),
        lax.all_gather(w_proj, "seq", axis=0, tiled=True),
        lax.all_gather(attention_vectors, "seq", axis=0, tiled=True),
        lax.all_gather(block_vectors, "seq", axis=0, tiled=True),
    )
    gathered = (
        lax.all_gather(part_qkv, "dp", axis=0, tiled=True),
        lax.all_gather(part_out, "dp", axis=0, tiled=True),
        lax.all_gather(part_fc, "dp", axis=0, tiled=True),
        lax.all_gather(part_proj, "dp", axis=0, tiled=True),
        lax.all_gather(part_first, "dp", axis=0, tiled=True),
        lax.all_gather(part_second, "dp", axis=0, tiled=True),
    )
    (
        query_key_value_weight,
        output_weight,
        expand_weight,
        contract_weight,
        token_rows,
        expand_bias,
    ) = split_weights(gathered, width)
    place = rank * count + jnp.arange(count)
    key_place = jnp.arange(span)
    allowed = (key_place[None, None, :] <= place[None, :, None]) & (
        key_place[None, None, :] < lengths[:, None, None]
    )
    valid = place[None, :] < lengths[:, None]
    source = tokens.astype(jnp.float32)
    normed_low = layer_norm(source, token_rows[0], token_rows[1]).astype(jnp.bfloat16)
    mixed_heads = jnp.einsum(
        "scd,de->sce", normed_low, query_key_value_weight, preferred_element_type=jnp.float32
    )
    query = (mixed_heads[..., :width] + token_rows[2]).astype(jnp.bfloat16)
    keys = mixed_heads[..., width : 2 * width].astype(jnp.bfloat16)
    values = (mixed_heads[..., 2 * width :] + token_rows[3]).astype(jnp.bfloat16)
    all_keys, all_values = (
        lax.all_gather(keys, "seq", axis=1, tiled=True),
        lax.all_gather(values, "seq", axis=1, tiled=True),
    )
    query_heads = to_heads(query, heads)
    key_heads = to_heads(all_keys, heads)
    value_heads = to_heads(all_values, heads)
    head_result, normal = lax.map(
        partial(head_forward, allowed), (query_heads, key_heads, value_heads)
    )
    attention_output = from_heads(head_result).astype(jnp.bfloat16)
    middle_state = (
        source
        + jnp.einsum(
            "scd,de->sce", attention_output, output_weight, preferred_element_type=jnp.float32
        )
        + token_rows[4]
    )
    second_normed = layer_norm(middle_state, token_rows[5], token_rows[6]).astype(jnp.bfloat16)
    inner_hidden = (
        jnp.einsum("scd,df->scf", second_normed, expand_weight, preferred_element_type=jnp.float32)
        + expand_bias
    )
    active_low = tanh_gelu(inner_hidden).astype(jnp.bfloat16)
    result = (
        middle_state
        + jnp.einsum("scf,fd->scd", active_low, contract_weight, preferred_element_type=jnp.float32)
        + token_rows[7]
    )
    output = result.astype(jnp.bfloat16)
    again_qkv, again_out, again_fc, again_proj, again_first, again_second = (
        lax.all_gather(w_qkv, "seq", axis=0, tiled=True),
        lax.all_gather(w_out, "seq", axis=0, tiled=True),
        lax.all_gather(w_fc, "seq", axis=0, tiled=True),
        lax.all_gather(w_proj, "seq", axis=0, tiled=True),
        lax.all_gather(attention_vectors, "seq", axis=0, tiled=True),
        lax.all_gather(block_vectors, "seq", axis=0, tiled=True),
    )
    again = (
        lax.all_gather(again_qkv, "dp", axis=0, tiled=True),
        lax.all_gather(again_out, "dp", axis=0, tiled=True),
        lax.all_gather(again_fc, "dp", axis=0, tiled=True),
        lax.all_gather(again_proj, "dp", axis=0, tiled=True),
        lax.all_gather(again_first, "dp", axis=0, tiled=True),
        lax.all_gather(again_second, "dp", axis=0, tiled=True),
    )
    (
        query_key_value_weight,
        output_weight,
        expand_weight,
        contract_weight,
        token_rows,
        expand_bias,
    ) = split_weights(again, width)
    grad_result = cotangent * valid.astype(jnp.bfloat16)[..., None]
    grad_wide = grad_result.astype(jnp.float32)
    grad_proj = jnp.einsum(
        "scf,scd->fd", active_low, grad_result, preferred_element_type=jnp.float32
    )
    bias_proj_grad = jnp.sum(grad_wide, axis=(0, 1))
    grad_active = jnp.einsum(
        "scd,fd->scf", grad_result, contract_weight, preferred_element_type=jnp.float32
    )
    gelu_back = jax.vjp(tanh_gelu, inner_hidden)[1]
    inner_low = gelu_back(grad_active)[0].astype(jnp.bfloat16)
    bias_fc_grad = jnp.sum(inner_low.astype(jnp.float32), axis=(0, 1))
    grad_fc = jnp.einsum(
        "scd,scf->df", second_normed, inner_low, preferred_element_type=jnp.float32
    )
    grad_fc_full = jnp.concatenate([grad_fc, bias_fc_grad[None, :]], axis=0).reshape(-1)
    grad_normed_two = jnp.einsum(
        "scf,df->scd", inner_low, expand_weight, preferred_element_type=jnp.float32
    )
    norm_two_back = jax.vjp(layer_norm, middle_state, token_rows[5], token_rows[6])[1]
    grad_mid, gain_two_grad, shift_two_grad = norm_two_back(grad_normed_two)
    grad_mid = grad_mid + grad_wide
    branch_low = grad_mid.astype(jnp.bfloat16)
    bias_out_grad = jnp.sum(branch_low.astype(jnp.float32), axis=(0, 1))
    grad_out_mat = jnp.einsum(
        "scd,sce->de", attention_output, branch_low, preferred_element_type=jnp.float32
    )
    grad_attended = jnp.einsum(
        "sce,de->scd", branch_low, output_weight, preferred_element_type=jnp.float32
    ).astype(jnp.bfloat16)
    grad_query, grad_keys, grad_values = lax.map(
        partial(head_backward, allowed),
        (query_heads, key_heads, value_heads, to_heads(grad_attended, heads), normal),
    )
    keys_sum, values_sum = (
        lax.psum_scatter(from_heads(grad_keys), "seq", scatter_dimension=1, tiled=True),
        lax.psum_scatter(from_heads(grad_values), "seq", scatter_dimension=1, tiled=True),
    )
    query_low = from_heads(grad_query).astype(jnp.bfloat16)
    keys_low = keys_sum.astype(jnp.bfloat16)
    values_low = values_sum.astype(jnp.bfloat16)
    bias_query_grad = jnp.sum(query_low.astype(jnp.float32), axis=(0, 1))
    bias_value_grad = jnp.sum(values_low.astype(jnp.float32), axis=(0, 1))
    grad_mixed = jnp.concatenate([query_low, keys_low, values_low], axis=-1)
    grad_qkv = jnp.einsum("scd,sce->de", normed_low, grad_mixed, preferred_element_type=jnp.float32)
    grad_normed = jnp.einsum(
        "sce,de->scd", grad_mixed, query_key_value_weight, preferred_element_type=jnp.float32
    )
    norm_one_back = jax.vjp(layer_norm, source, token_rows[0], token_rows[1])[1]
    grad_source, gain_one_grad, shift_one_grad = norm_one_back(grad_normed)
    input_grad = grad_mid + grad_source
    first_grad = jnp.concatenate([gain_one_grad, shift_one_grad, bias_query_grad, bias_value_grad])
    second_grad = jnp.concatenate([bias_out_grad, gain_two_grad, shift_two_grad, bias_proj_grad])
    qkv_part, out_part, fc_part, proj_part, first_part, second_part = (
        lax.psum_scatter(grad_qkv.reshape(-1), "dp", scatter_dimension=0, tiled=True),
        lax.psum_scatter(grad_out_mat.reshape(-1), "dp", scatter_dimension=0, tiled=True),
        lax.psum_scatter(grad_fc_full, "dp", scatter_dimension=0, tiled=True),
        lax.psum_scatter(grad_proj.reshape(-1), "dp", scatter_dimension=0, tiled=True),
        lax.psum_scatter(first_grad, "dp", scatter_dimension=0, tiled=True),
        lax.psum_scatter(second_grad, "dp", scatter_dimension=0, tiled=True),
    )
    qkv_shard, out_shard, fc_shard, proj_shard, first_shard, second_shard = (
        lax.psum_scatter(qkv_part, "seq", scatter_dimension=0, tiled=True),
        lax.psum_scatter(out_part, "seq", scatter_dimension=0, tiled=True),
        lax.psum_scatter(fc_part, "seq", scatter_dimension=0, tiled=True),
        lax.psum_scatter(proj_part, "seq", scatter_dimension=0, tiled=True),
        lax.psum_scatter(first_part, "seq", scatter_dimension=0, tiled=True),
        lax.psum_scatter(second_part, "seq", scatter_dimension=0, tiled=True),
    )
    return (
        output,
        input_grad,
        qkv_shard,
        out_shard,
        fc_shard,
        proj_shard,
        first_shard,
        second_shard,
    )


def solution(mesh):
    in_specs = (
        P("dp", "seq", None),
        P("dp", "seq", None),
        P("dp"),
        P(("dp", "seq")),
        P(("dp", "seq")),
        P(("dp", "seq")),
        P(("dp", "seq")),
        P(("dp", "seq")),
        P(("dp", "seq")),
    )
    out_specs = (
        P("dp", "seq", None),
        P("dp", "seq", None),
        P(("dp", "seq")),
        P(("dp", "seq")),
        P(("dp", "seq")),
        P(("dp", "seq")),
        P(("dp", "seq")),
        P(("dp", "seq")),
    )
    return jax.shard_map(local, mesh=mesh, in_specs=in_specs, out_specs=out_specs, check_vma=False)
```

profile of v0, /device:TPU:0, one launch (start us, length us, event | category | flops | bytes accessed | tf_op | source)
XLA Modules:
  0.0 6387.4 jit_solution(10073918586808207974)
XLA Ops:
  7.2 6.3 reshape.576
  15.8 5.9 dynamic-update-slice.4
  23.4 25.4 all-gather.19.cloned.1.call-done
  49.0 8.1 reshape.584
  57.3 19.0 all-gather.2
  77.1 40.4 all-reduce.29.cloned.1.call-done
  117.4 7.4 broadcast.247
  124.8 39.2 dynamic-update-slice.5
  166.0 6.0 all-reduce.23
  172.5 51.9 all-reduce.22
  226.2 478.7 %all-gather.21.cloned.1.call-done = bf16[8,1,960000]{2,1,0:T(2,128)(2,1)} async-done(((bf16[1,1,960000]{2,1,0:T(2,128)(2,1)}), bf16[8,1,960000]{2,1,0:T(2,128)(2,1)}) %all-gather.21.cloned.1.call-update) | async-done | bytes 15360016 | tf_op jit(solution)/shard_map/all_gather | solution.py:95
  704.9 325.4 %reduce.24 = bf16[8,960000]{1,0:T(8,128)(2,1)} reduce(bf16[8,1,960000]{2,1,0:T(2,128)(2,1)} %all-gather.21.cloned.1.call-done, bf16[]{:T(256)} %constant.172), dimensions={1}, to_apply=%all-gather.1.reduce_sub_computation | reduce | bytes 30720002 | tf_op jit(solution)/shard_map/all_gather | solution.py:95
  1030.3 34.2 reshape.626
  1064.5 25.2 reshape.541
  1089.7 14.8 convolution_bitcast_fusion.4
  1104.5 2.4 slice.98
  1107.0 3.3 fusion.72
  1110.4 17.7 reduce.26
  1128.1 4.2 reshape.585
  1133.1 32.0 reduce.25
  1165.2 12.3 reshape.628
  1177.5 9.6 reshape.545
  1187.1 325.9 %all-reduce.31.cloned.1.call-done = bf16[10246400]{0:T(1024)(128)(2,1)} async-done(((bf16[10246400]{0:T(1024)(128)(2,1)}), bf16[10246400]{0:T(1024)(128)(2,1)}) %all-reduce.31.cloned.1.call-update) | async-done | bytes 20492816
  1513.1 16.9 slice.87
  1530.0 35.4 slice.74
  1566.1 1.9 copy.26
  1568.0 7.0 copy.27
  1576.0 7.1 copy.28
  1583.3 79.7 %while.28 = (s32[]{:T(128)}, bf16[25,1,256,64]{2,3,1,0:T(8,128)(2,1)S(1)}, f32[25,1,256]{2,1,0:T(1,128)S(1)}, bf16[25,1,256,64]{3,2,1,0:T(8,128)(2,1)}, bf16[25,...) while((s32[]{:T(128)}, ...), condition=%wide.region_5.6_spmd.clone, body=%wide.region_2.5_spmd.clone.sunk | while | flops 69730048 | bytes 3815529 | solution.py:131
  1663.0 5.3 fusion.110
  1668.6 12.4 convolution_add_fusion
  1681.0 289.2 %all-gather.17.cloned.1.call-done = bf16[10240000]{0:T(1024)(128)(2,1)} async-done(((bf16[1280000]{0:T(1024)(128)(2,1)}), bf16[10240000]{0:T(1024)(128)(2,1)}) %all-gather.17.cloned.1.call-update) | async-done | bytes 20480016 | tf_op jit(solution)/shard_map/all_gather | solution.py:98
  1970.3 34.0 reshape.547
  2004.2 14.1 convert_reduce_fusion
  2018.3 13.4 fusion.74
  2033.5 4.5 convolution_convert_fusion
  2039.8 200.8 %while.29 = (s32[]{:T(128)}, bf16[25,1,256,64]{2,3,1,0:T(8,128)(2,1)S(1)}, f32[25,1,1024,64]{2,3,1,0:T(8,128)}, f32[25,1,1024,64]{2,3,1,0:T(8,128)}, bf16[25,1,2...) while((s32[]{:T(128)}, ...), condition=%wide.region_12.13_spmd.clone, body=%wide.region_10.12_spmd.clone.sunk | while | flops 171179776 | bytes 9515137 | solution.py:208
  2236.9 1.8 fusion.156
  2241.4 22.7 fusion.84
  2264.1 48.3 reshape.557
  2312.4 7.0 fusion.81
  2319.4 13.5 reshape.555
  2332.8 18.4 fusion.101
  2351.2 28.1 pad_maximum_fusion
  2379.3 39.9 reshape.556
  2419.3 2.5 convert_element_type.144
  2424.4 13.8 fusion.77
  2438.2 36.5 reshape.554
  2477.1 3609.6 %all-reduce.33.cloned.1.call-done = (f32[7680000]{0:T(1024)}, f32[2560000]{0:T(1024)}, f32[10246400]{0:T(1024)}, f32[10240000]{0:T(1024)}) async-done(((f32[7680000]{0:T(1024)}, f32[2560000]{0:T(1024)}, f32[10246400]{0:T(1024)}, f32[10240000]{0:T(1024)}), (f32[7680000]{0:T(1024)}, f32[2560000]{0:T(1024)}, f32[10246400]{0:T(1024)}, f32[10240000]{0:T(1024)})) %all-reduce.33.cloned.1.call-update) | async-done | bytes 122905616
  6086.8 5.1 dynamic-slice.7
  6091.9 2.8 dynamic-slice.11
  6094.6 4.4 dynamic-slice.19
  6099.0 4.8 dynamic-slice.15
  6107.8 2.2 reduce_sum.199
  6110.5 17.3 fusion.60
  6127.8 8.2 fusion.71
  6137.3 35.6 all-reduce.18
  6173.1 6.4 all-reduce.20
  6180.8 3.3 add_add_fusion.2
  6184.1 186.5 %all-reduce.35.cloned.1.call-done = (f32[960000]{0:T(1024)}, f32[320000]{0:T(1024)}, f32[1280800]{0:T(1024)}, f32[1280000]{0:T(1024)}) async-done(((f32[960000]{0:T(1024)}, f32[320000]{0:T(1024)}, f32[1280800]{0:T(1024)}, f32[1280000]{0:T(1024)}), (f32[960000]{0:T(1024)}, f32[320000]{0:T(1024)}, f32[1280800]{0:T(1024)}, f32[1280000]{0:T(1024)})) %all-reduce.35.cloned.1.call-update) | async-done | bytes 15363216
  6370.6 2.5 dynamic-slice.9
  6373.1 1.8 dynamic-slice.13
  6374.9 2.8 dynamic-slice.17
  6377.7 2.8 dynamic-slice.21
  (449 shorter events, 296.4 us)
Async XLA Ops:
  7.2 8.7 copy-start.12
  7.2 41.7 all-gather.19.cloned.1.call-start
  13.5 103.9 %all-reduce.29.cloned.1.call-start = ((), (), s32[]{:S(2)}) async-start(), calls=%async_computation.7 | async-start | bytes 5124096
  21.7 1.6 copy-start.3
  21.7 27.2 copy-start.13
  23.4 681.5 %all-gather.21.cloned.1.call-start = ((), (), s32[]{:S(2)}) async-start(), calls=%async_computation.10 | async-start | bytes 34560000 | tf_op jit(solution)/shard_map/all_gather | solution.py:95
  48.9 8.2 copy-start.16
  48.9 1061.5 %all-gather.25.cloned.1.call-start = ((), (), s32[]{:S(2)}) async-start(), calls=%async_computation.12 | async-start | bytes 6400000 | tf_op jit(solution)/shard_map/all_gather | solution.py:90
  57.1 1076.1 %all-gather.23.cloned.1.call-start = ((), (), s32[]{:S(2)}) async-start(), calls=%async_computation.11 | async-start | bytes 11520000 | tf_op jit(solution)/shard_map/all_gather | solution.py:96
  76.4 1436.7 %all-reduce.31.cloned.1.call-start = ((), (), s32[]{:S(2)}) async-start(), calls=%async_computation.8 | async-start | bytes 40988672
  117.4 7.4 copy-start.11
  164.0 1.5 copy-start.33
  164.0 1.7 copy-start.34
  164.0 60.4 copy-start
  164.0 1403.9 %all-gather.13.cloned.1.call-start = ((), (), s32[]{:S(2)}) async-start(), calls=%async_computation.2 | async-start | bytes 4096000 | tf_op jit(solution)/shard_map/all_gather | solution.py:125
  224.6 865.1 %copy-start.19 = (f32[256]{0:T(256)}, f32[256]{0:T(256)S(1)}, u32[]{:S(2)}) copy-start(f32[256]{0:T(256)S(1)} %broadcast_multiply_fusion.1) | copy-start | bytes 3076
  224.9 0.6 copy-start.27
  224.9 864.8 %copy-start.21 = (f32[256]{0:T(256)}, f32[256]{0:T(256)S(1)}, u32[]{:S(2)}) copy-start(f32[256]{0:T(256)S(1)} %fusion.95) | copy-start | bytes 3076
  226.2 863.5 %copy-start.14 = (f32[1600]{0:T(1024)}, f32[1600]{0:T(1024)S(1)}, u32[]{:S(2)}) copy-start(f32[1600]{0:T(1024)S(1)} %get-tuple-element.229) | copy-start | bytes 19204
  226.2 863.6 %copy-start.17 = (f32[1600]{0:T(1024)}, f32[1600]{0:T(1024)S(1)}, u32[]{:S(2)}) copy-start(f32[1600]{0:T(1024)S(1)} %get-tuple-element.228) | copy-start | bytes 19204
  1107.0 469.1 %all-gather.15.cloned.1.call-start = ((), (), s32[]{:S(2)}) async-start(), calls=%async_computation.3 | async-start | bytes 4096000 | tf_op jit(solution)/shard_map/all_gather | solution.py:126
  1110.4 859.9 %all-gather.17.cloned.1.call-start = ((), (), s32[]{:S(2)}) async-start(), calls=%async_computation.4 | async-start | bytes 23040000 | tf_op jit(solution)/shard_map/all_gather | solution.py:98
  1132.3 1286.9 %reduce-scatter.3.cloned.1.call-start = ((), (), s32[]{:S(2)}) async-start(), calls=%async_computation.5 | async-start | bytes 8192000 | tf_op jit(solution)/shard_map/reduce_scatter | solution.py:213
  1133.1 1108.3 %copy-start.31 = (bf16[256]{0:T(256)(128)(2,1)}, bf16[256]{0:T(256)(128)(2,1)S(1)}, u32[]{:S(2)}) copy-start(bf16[256]{0:T(256)(128)(2,1)S(1)} %compare_convert_fusion) | copy-start | bytes 1540
  1663.0 5.3 copy-start.7
  1681.0 323.2 %copy-start.4 = (bf16[1,256,1600]{1,2,0:T(8,128)(2,1)S(1)}, bf16[1,256,1600]{1,2,0:T(8,128)(2,1)}, u32[]{:S(2)}) copy-start(bf16[1,256,1600]{1,2,0:T(8,128)(2,1)} %param.14) | copy-start | bytes 2457604
  2031.7 1.7 copy-start.6
  2032.2 5.7 copy-start.2
  2032.2 5.7 copy-start.25
  2033.5 4.5 copy-start.10
  2240.6 181.1 %reduce-scatter.5.cloned.1.call-start = ((), (), s32[]{:S(2)}) async-start(), calls=%async_computation.6 | async-start | bytes 8192000 | tf_op jit(solution)/shard_map/reduce_scatter | solution.py:214
  2241.3 3845.4 %all-reduce.33.cloned.1.call-start = ((), (), s32[]{:S(2)}) async-start(), calls=%async_computation.13 | async-start | bytes 245817344
  2264.1 48.3 copy-start.8
  2419.2 5.2 copy-start.1
  2419.2 5.2 copy-start.15
  2419.2 5.2 copy-start.18
  2419.2 5.2 copy-start.20
  2419.2 5.2 copy-start.22
  2423.5 0.9 copy-start.9
  2474.8 3895.8 %all-reduce.35.cloned.1.call-start = ((), (), s32[]{:S(2)}) async-start(), calls=%async_computation.14 | async-start | bytes 30736384
  6103.8 6.6 copy-start.23
  6103.8 6.6 copy-start.24
  6103.8 6.6 copy-start.30
  6103.8 6.7 copy-start.29
  6127.8 8.6 copy-start.28
  6136.0 44.8 copy-start.5
  6136.0 44.8 copy-start.26
  6136.1 44.7 copy-start.32
Sparse Core Ops, SparseCore 0:
  13.6 35.2 all-gather.18
  51.3 66.0 all-reduce.28
  119.0 585.7 all-gather.20
  706.9 39.7 all-gather.24
  749.0 147.8 all-gather.22
  901.4 611.6 all-reduce.30
  1515.3 28.8 all-gather.12
  1546.3 29.6 all-gather.14
  1577.7 392.5 all-gather.16
  2240.7 60.0 reduce-scatter.2
  2303.4 60.0 reduce-scatter.4
  2474.9 3611.7 all-reduce.32
  6103.9 266.6 all-reduce.34
where the time goes:
time: 6410 us; the launch traced here: 6390 us
  waiting for transfers between devices  4960 us (77%)
  other arithmetic  434 us (7%)
  local copies, waits for them, and re-layouts  433 us (7%)
  matrix products  418 us (7%)
  blocking collectives  119 us (2%)
    unnamed x17, waiting for transfers between devices  4160 us
    all_gather x1, waiting for transfers between devices, local(): lax.all_gather(part_qkv, 'dp', axis=0, tiled=True)  479 us
    all_gather x1, other arithmetic, local(): lax.all_gather(part_qkv, 'dp', axis=0, tiled=True)  325 us
    all_gather x1, waiting for transfers between devices, local(): lax.all_gather(part_proj, 'dp', axis=0, tiled=True)  289 us
    unnamed x101, local copies, waits for them, and re-layouts  152 us
  transfers between devices with their start and end apart: 13, of which 8 were waited for; matrix products, arithmetic and copies ran while one was open for 15% of the time, Pallas kernels for 0%

commit v1 on v0

--- a/solution.py
+++ b/solution.py
@@ -6,6 +6,19 @@
 
 HD = 64
 EPS = 1e-05
+
+
+def ring_gather(shard, axis, dim):
+    ways = lax.axis_size(axis)
+    up = [(d, (d + 1) % ways) for d in range(ways)]
+    down = [(d, (d - 1) % ways) for d in range(ways)]
+    earlier, later = ([shard], [shard])
+    for _ in range(ways // 2):
+        earlier.append(lax.ppermute(earlier[-1], axis, up))
+    for _ in range((ways - 1) // 2):
+        later.append(lax.ppermute(later[-1], axis, down))
+    line = jnp.concatenate([*earlier[::-1], *later[1:]], axis=dim)
+    return jnp.roll(line, (lax.axis_index(axis) - ways // 2) * shard.shape[dim], axis=dim)
 
 
 def layer_norm(value, gain, shift):
@@ -92,7 +105,7 @@
         lax.all_gather(block_vectors, "seq", axis=0, tiled=True),
     )
     gathered = (
-        lax.all_gather(part_qkv, "dp", axis=0, tiled=True),
+        ring_gather(part_qkv, "dp", 0),
         lax.all_gather(part_out, "dp", axis=0, tiled=True),
         lax.all_gather(part_fc, "dp", axis=0, tiled=True),
         lax.all_gather(part_proj, "dp", axis=0, tiled=True),

time: 6410 us -> 7350 us (1.15)
  local copies, waits for them, and re-layouts: 433 us -> 957 us
  waiting for transfers between devices: 4960 us -> 5210 us
    unnamed x101 -> x125, local copies, waits for them, and re-layouts: 152 us -> 608 us
    ppermute x0 -> x7, waiting for transfers between devices: none -> 259 us  [the longest x4 252 us: ring_gather(): earlier.append(lax.ppermute(earlier[-1], axis, up))]
    unnamed x17, waiting for transfers between devices: 4160 us -> 4060 us
    all_gather x1, waiting for transfers between devices: 479 us -> 564 us  [local(): lax.all_gather(again_qkv, 'dp', axis=0, tiled=True)]
    all_gather x1 -> x2, other arithmetic: 325 us -> 362 us  [the longest x1 325 us: local(): lax.all_gather(again_qkv, 'dp', axis=0, tiled=True)]
  transfers between devices with their start and end apart: 13 -> 20, of which waited for: 8 -> 9; matrix products, arithmetic and copies ran while one was open for 15% -> 21% of each run, Pallas kernels for 0% -> 0%
where the time goes in v1:
time: 7350 us; the launch traced here: 7280 us
  waiting for transfers between devices  5210 us (71%)
  local copies, waits for them, and re-layouts  957 us (13%)
  other arithmetic  469 us (6%)
  matrix products  417 us (6%)
  blocking collectives  155 us (2%)
    unnamed x17, waiting for transfers between devices  4060 us
    unnamed x125, local copies, waits for them, and re-layouts  608 us
    all_gather x1, waiting for transfers between devices, local(): lax.all_gather(again_qkv, 'dp', axis=0, tiled=True)  564 us
    all_gather x1, waiting for transfers between devices, local(): lax.all_gather(part_proj, 'dp', axis=0, tiled=True)  328 us
    all_gather x1, other arithmetic, local(): lax.all_gather(again_qkv, 'dp', axis=0, tiled=True)  325 us
    ppermute x4, waiting for transfers between devices, ring_gather(): earlier.append(lax.ppermute(earlier[-1], axis, up))  252 us
  transfers between devices with their start and end apart: 20, of which 9 were waited for; matrix products, arithmetic and copies ran while one was open for 21% of the time, Pallas kernels for 0%

profile of v1, /device:TPU:0, one launch (start us, length us, event | category | flops | bytes accessed | tf_op | source)
XLA Modules:
  0.0 7280.3 jit_solution(2126792709130679528)
XLA Ops:
  23.3 7.7 reshape.585
  31.3 20.2 all-gather.1
  55.7 37.1 reduce.24
  98.6 45.4 collective-permute-done
  150.1 91.1 %collective-permute-done.1 = bf16[960000]{0:T(1024)(128)(2,1)S(1)} collective-permute-done((bf16[960000]{0:T(1024)(128)(2,1)S(1)}, bf16[960000]{0:T(1024)(128)(2,1)S(1)}, u32[]{:S(2)}, u32[]{:S(2)}) %collective-permute-start.1) | collective-permute-done | bytes 1920032 | tf_op jit(solution)/shard_map/ppermute | solution.py:17
  251.2 115.6 %collective-permute-done.2 = bf16[960000]{0:T(1024)(128)(2,1)} collective-permute-done((bf16[960000]{0:T(1024)(128)(2,1)S(1)}, bf16[960000]{0:T(1024)(128)(2,1)}, u32[]{:S(2)}, u32[]{:S(2)}) %collective-permute-start.2) | collective-permute-done | bytes 1920032 | tf_op jit(solution)/shard_map/ppermute | solution.py:17
  369.4 7.1 collective-permute-done.5
  376.4 24.5 collective-permute-start.6
  402.8 7.3 all-reduce.23
  410.6 84.8 %all-reduce.22 = (bf16[6400]{0:T(1024)(128)(2,1)S(1)}, bf16[6400]{0:T(1024)(128)(2,1)S(1)}) all-reduce(bf16[6400]{0:T(1024)(128)(2,1)S(1)} %dynamic-update-slice.3, bf16[6400]{0:T(1024)(128)(2,1)S(1)} %dynamic-update-slice.1), channel_id=1, replica_groups=mesh['dp'=8,'seq'=4] {'dp'}, use_global_device_ids=true, to_apply=%add.3 | all-reduce | flops 12800 | bytes 51200
  497.2 30.0 dynamic-update-slice.6
  527.2 29.9 dynamic-update-slice.7
  557.1 30.0 dynamic-update-slice.8
  587.1 30.0 dynamic-update-slice.9
  617.1 29.9 dynamic-update-slice.10
  647.1 30.0 dynamic-update-slice.11
  677.1 29.9 dynamic-update-slice.12
  707.0 30.0 dynamic-update-slice.13
  737.1 30.0 dynamic-update-slice.14
  767.1 29.9 dynamic-update-slice.15
  797.0 30.0 dynamic-update-slice.16
  827.1 29.8 dynamic-update-slice.17
  856.9 30.0 dynamic-update-slice.18
  886.9 30.0 dynamic-update-slice.19
  916.9 29.9 dynamic-update-slice.20
  946.8 30.0 dynamic-update-slice.21
  976.8 13.0 dynamic_slice.31
  989.8 25.1 reshape.543
  1014.9 14.7 convolution_bitcast_fusion.4
  1036.1 7.5 broadcast.247
  1043.7 39.9 dynamic-update-slice.5
  1084.0 17.6 reduce.26
  1107.4 31.8 reduce.25
  1139.3 12.4 reshape.630
  1151.7 9.6 reshape.547
  1162.9 7.2 copy.27
  1170.1 7.1 copy.28
  1177.2 80.1 %while.28 = (s32[]{:T(128)}, bf16[25,1,256,64]{2,3,1,0:T(8,128)(2,1)S(1)}, f32[25,1,256]{2,1,0:T(1,128)S(1)}, bf16[25,1,256,64]{3,2,1,0:T(8,128)(2,1)}, bf16[25,...) while((s32[]{:T(128)}, ...), condition=%wide.region_5.6_spmd.clone, body=%wide.region_2.5_spmd.clone.sunk | while | flops 69730048 | bytes 3815529 | solution.py:144
  1262.8 447.9 %all-reduce.31.cloned.1.call-done = bf16[10246400]{0:T(1024)(128)(2,1)} async-done(((bf16[10246400]{0:T(1024)(128)(2,1)}), bf16[10246400]{0:T(1024)(128)(2,1)}) %all-reduce.31.cloned.1.call-update) | async-done | bytes 20492816
  1710.7 17.1 slice.87
  1727.8 35.3 slice.74
  1763.9 12.4 convolution_add_fusion
  1776.3 327.7 %all-gather.17.cloned.1.call-done = bf16[10240000]{0:T(1024)(128)(2,1)} async-done(((bf16[1280000]{0:T(1024)(128)(2,1)}), bf16[10240000]{0:T(1024)(128)(2,1)}) %all-gather.17.cloned.1.call-update) | async-done | bytes 20480016 | tf_op jit(solution)/shard_map/all_gather | solution.py:111
  2104.0 33.9 reshape.549
  2138.0 14.0 convert_reduce_fusion
  2152.0 13.4 fusion.74
  2173.5 200.8 %while.29 = (s32[]{:T(128)}, bf16[25,1,256,64]{2,3,1,0:T(8,128)(2,1)S(1)}, f32[25,1,1024,64]{2,3,1,0:T(8,128)}, f32[25,1,1024,64]{2,3,1,0:T(8,128)}, bf16[25,1,2...) while((s32[]{:T(128)}, ...), condition=%wide.region_12.13_spmd.clone, body=%wide.region_10.12_spmd.clone.sunk | while | flops 171179776 | bytes 9515137 | solution.py:221
  2375.0 22.9 fusion.84
  2397.9 48.4 reshape.560
  2446.3 7.2 fusion.81
  2453.4 13.5 reshape.558
  2466.9 18.4 fusion.101
  2485.3 28.1 pad_maximum_fusion
  2513.4 39.9 reshape.559
  2557.0 12.9 fusion.77
  2569.9 36.5 reshape.557
  2609.6 3608.5 %all-reduce.33.cloned.1.call-done = (f32[7680000]{0:T(1024)}, f32[2560000]{0:T(1024)}, f32[10246400]{0:T(1024)}, f32[10240000]{0:T(1024)}) async-done(((f32[7680000]{0:T(1024)}, f32[2560000]{0:T(1024)}, f32[10246400]{0:T(1024)}, f32[10240000]{0:T(1024)}), (f32[7680000]{0:T(1024)}, f32[2560000]{0:T(1024)}, f32[10246400]{0:T(1024)}, f32[10240000]{0:T(1024)})) %all-reduce.33.cloned.1.call-update) | async-done | bytes 122905616
  6239.0 564.4 %all-gather.25.cloned.1.call-done = bf16[8,1,960000]{2,1,0:T(2,128)(2,1)} async-done(((bf16[1,1,960000]{2,1,0:T(2,128)(2,1)}), bf16[8,1,960000]{2,1,0:T(2,128)(2,1)}) %all-gather.25.cloned.1.call-update) | async-done | bytes 15360016 | tf_op jit(solution)/shard_map/all_gather | solution.py:176
  6803.4 325.3 %reduce.27 = bf16[8,960000]{1,0:T(8,128)(2,1)} reduce(bf16[8,1,960000]{2,1,0:T(2,128)(2,1)} %all-gather.25.cloned.1.call-done, bf16[]{:T(256)} %constant.200), dimensions={1}, to_apply=%all-gather.4.reduce_sub_computation | reduce | bytes 30720002 | tf_op jit(solution)/shard_map/all_gather | solution.py:176
  7128.7 33.8 reshape.632
  7162.6 25.2 reshape.556
  7190.0 17.3 fusion.60
  7207.3 8.1 fusion.71
  7216.8 36.4 all-reduce.18
  (492 shorter events, 399.5 us)
Async XLA Ops:
  7.2 8.7 copy-start.17
  7.2 48.6 all-gather.19.cloned.1.call-start
  13.5 1022.6 %all-reduce.29.cloned.1.call-start = ((), (), s32[]{:S(2)}) async-start(), calls=%async_computation.7 | async-start | bytes 5124096
  15.8 15.3 copy-start.20
  21.7 1.5 copy-start.5
  23.3 1060.8 %all-gather.23.cloned.1.call-start = ((), (), s32[]{:S(2)}) async-start(), calls=%async_computation.11 | async-start | bytes 6400000 | tf_op jit(solution)/shard_map/all_gather | solution.py:103
  31.1 1076.3 %all-gather.21.cloned.1.call-start = ((), (), s32[]{:S(2)}) async-start(), calls=%async_computation.10 | async-start | bytes 11520000 | tf_op jit(solution)/shard_map/all_gather | solution.py:109
  51.5 1111.4 %all-gather.13.cloned.1.call-start = ((), (), s32[]{:S(2)}) async-start(), calls=%async_computation.2 | async-start | bytes 4096000 | tf_op jit(solution)/shard_map/all_gather | solution.py:138
  92.9 309.4 %copy-start.37 = (bf16[200]{0:T(256)(128)(2,1)S(1)}, bf16[200]{0:T(256)(128)(2,1)}, u32[]{:S(2)}) copy-start(bf16[200]{0:T(256)(128)(2,1)} %param.21) | copy-start | bytes 1204
  92.9 309.7 %copy-start.38 = (bf16[200]{0:T(256)(128)(2,1)S(1)}, bf16[200]{0:T(256)(128)(2,1)}, u32[]{:S(2)}) copy-start(bf16[200]{0:T(256)(128)(2,1)} %param.20) | copy-start | bytes 1204
  92.9 402.5 %copy-start.2 = (bf16[1,256,1600]{1,2,0:T(8,128)(2,1)S(1)}, bf16[1,256,1600]{1,2,0:T(8,128)(2,1)}, u32[]{:S(2)}) copy-start(bf16[1,256,1600]{1,2,0:T(8,128)(2,1)} %param.13) | copy-start | bytes 2457604
  97.2 46.9 collective-permute-start
  144.1 1.3 copy-start.6
  145.4 95.9 %collective-permute-start.1 = (bf16[960000]{0:T(1024)(128)(2,1)S(1)}, bf16[960000]{0:T(1024)(128)(2,1)S(1)}, u32[]{:S(2)}, u32[]{:S(2)}) collective-permute-start(bf16[960000]{0:T(1024)(128)(2,1)S(1)} %collective-permute-done), channel_id=1, source_target_pairs={{0,4},{4,8},{8,12},{12,16},{16,20},{20,24},{24,28},{28,0},{1,5},{5... | collective-permute-start | bytes 5760008 | tf_op jit(solution)/shard_map/ppermute | solution.py:17
  145.4 98.3 %collective-permute-start.4 = (bf16[960000]{0:T(1024)(128)(2,1)}, bf16[960000]{0:T(1024)(128)(2,1)S(1)}, u32[]{:S(2)}, u32[]{:S(2)}) collective-permute-start(bf16[960000]{0:T(1024)(128)(2,1)} %reshape.580), channel_id=1, source_target_pairs={{0,28},{4,0},{8,4},{12,8},{16,12},{20,16},{24,20},{28,24},{1,29},{... | collective-permute-start | bytes 5760008 | tf_op jit(solution)/shard_map/ppermute | solution.py:19
  241.2 135.2 %copy-start.8 = (bf16[960000]{0:T(1024)(128)(2,1)}, bf16[960000]{0:T(1024)(128)(2,1)S(1)}, u32[]{:S(2)}) copy-start(bf16[960000]{0:T(1024)(128)(2,1)S(1)} %collective-permute-done.1) | copy-start | bytes 5760004
  241.2 125.5 %collective-permute-start.2 = (bf16[960000]{0:T(1024)(128)(2,1)S(1)}, bf16[960000]{0:T(1024)(128)(2,1)}, u32[]{:S(2)}, u32[]{:S(2)}) collective-permute-start(bf16[960000]{0:T(1024)(128)(2,1)S(1)} %collective-permute-done.1), channel_id=1, source_target_pairs={{0,4},{4,8},{8,12},{12,16},{16,20},{20,24},{24,28},{28,0},{1,5},{5... | collective-permute-start | bytes 5760008 | tf_op jit(solution)/shard_map/ppermute | solution.py:17
  243.7 1.3 copy-start.7
  245.0 131.4 %collective-permute-start.5 = (bf16[960000]{0:T(1024)(128)(2,1)S(1)}, bf16[960000]{0:T(1024)(128)(2,1)}, u32[]{:S(2)}, u32[]{:S(2)}) collective-permute-start(bf16[960000]{0:T(1024)(128)(2,1)S(1)} %collective-permute-done.4), channel_id=1, source_target_pairs={{0,28},{4,0},{8,4},{12,8},{16,12},{20,16},{24,20},{28,24},{1,29},{... | collective-permute-start | bytes 5760008 | tf_op jit(solution)/shard_map/ppermute | solution.py:19
  366.8 130.4 %collective-permute-start.3 = (bf16[960000]{0:T(1024)(128)(2,1)}, bf16[960000]{0:T(1024)(128)(2,1)}, u32[]{:S(2)}, u32[]{:S(2)}) collective-permute-start(bf16[960000]{0:T(1024)(128)(2,1)} %collective-permute-done.2), channel_id=1, source_target_pairs={{0,4},{4,8},{8,12},{12,16},{16,20},{20,24},{24,28},{28,0},{1,5},{5... | collective-permute-start | bytes 5760008 | tf_op jit(solution)/shard_map/ppermute | solution.py:17
  376.4 330.6 %collective-permute-start.6 = (bf16[960000]{0:T(1024)(128)(2,1)}, bf16[960000]{0:T(1024)(128)(2,1)}, u32[]{:S(2)}, u32[]{:S(2)}) collective-permute-start(bf16[960000]{0:T(1024)(128)(2,1)} %collective-permute-done.5), channel_id=1, source_target_pairs={{0,28},{4,0},{8,4},{12,8},{16,12},{20,16},{24,20},{28,24},{1,29},{... | collective-permute-start | bytes 5760008 | tf_op jit(solution)/shard_map/ppermute | solution.py:19
  495.6 519.3 %copy-start.23 = (f32[256]{0:T(256)}, f32[256]{0:T(256)S(1)}, u32[]{:S(2)}) copy-start(f32[256]{0:T(256)S(1)} %broadcast_multiply_fusion.1) | copy-start | bytes 3076
  495.9 0.6 copy-start.31
  495.9 519.0 %copy-start.25 = (f32[256]{0:T(256)}, f32[256]{0:T(256)S(1)}, u32[]{:S(2)}) copy-start(f32[256]{0:T(256)S(1)} %fusion.95) | copy-start | bytes 3076
  497.2 517.7 %copy-start.18 = (f32[1600]{0:T(1024)}, f32[1600]{0:T(1024)S(1)}, u32[]{:S(2)}) copy-start(f32[1600]{0:T(1024)S(1)} %get-tuple-element.229) | copy-start | bytes 19204
  497.2 517.7 %copy-start.21 = (f32[1600]{0:T(1024)}, f32[1600]{0:T(1024)S(1)}, u32[]{:S(2)}) copy-start(f32[1600]{0:T(1024)S(1)} %get-tuple-element.228) | copy-start | bytes 19204
  1032.1 138.0 %all-gather.15.cloned.1.call-start = ((), (), s32[]{:S(2)}) async-start(), calls=%async_computation.3 | async-start | bytes 4096000 | tf_op jit(solution)/shard_map/all_gather | solution.py:139
  1035.4 675.3 %all-reduce.31.cloned.1.call-start = ((), (), s32[]{:S(2)}) async-start(), calls=%async_computation.8 | async-start | bytes 40988672
  1083.6 1020.5 %all-gather.17.cloned.1.call-start = ((), (), s32[]{:S(2)}) async-start(), calls=%async_computation.4 | async-start | bytes 23040000 | tf_op jit(solution)/shard_map/all_gather | solution.py:111
  1106.6 1446.7 %reduce-scatter.3.cloned.1.call-start = ((), (), s32[]{:S(2)}) async-start(), calls=%async_computation.5 | async-start | bytes 8192000 | tf_op jit(solution)/shard_map/reduce_scatter | solution.py:226
  1107.4 1267.6 %copy-start.35 = (bf16[256]{0:T(256)(128)(2,1)}, bf16[256]{0:T(256)(128)(2,1)S(1)}, u32[]{:S(2)}) copy-start(bf16[256]{0:T(256)(128)(2,1)S(1)} %compare_convert_fusion) | copy-start | bytes 1540
  1257.3 5.2 copy-start.12
  1262.5 1204.4 %copy-start = (f32[1,256,1600]{1,2,0:T(8,128)}, f32[1,256,1600]{1,2,0:T(8,128)S(1)}, u32[]{:S(2)}) copy-start(f32[1,256,1600]{1,2,0:T(8,128)S(1)} %get-tuple-element.235) | copy-start | bytes 4915204
  1776.3 361.7 %copy-start.9 = (bf16[1,256,1600]{1,2,0:T(8,128)(2,1)S(1)}, bf16[1,256,1600]{1,2,0:T(8,128)(2,1)}, u32[]{:S(2)}) copy-start(bf16[1,256,1600]{1,2,0:T(8,128)(2,1)} %param.14) | copy-start | bytes 2457604
  2165.4 1.7 copy-start.11
  2165.9 5.7 copy-start.4
  2165.9 5.7 copy-start.29
  2167.2 4.5 copy-start.16
  2374.3 180.6 %reduce-scatter.5.cloned.1.call-start = ((), (), s32[]{:S(2)}) async-start(), calls=%async_computation.6 | async-start | bytes 8192000 | tf_op jit(solution)/shard_map/reduce_scatter | solution.py:227
  2374.9 3843.2 %all-reduce.33.cloned.1.call-start = ((), (), s32[]{:S(2)}) async-start(), calls=%async_computation.13 | async-start | bytes 245817344
  2397.9 48.4 copy-start.13
  2553.3 3.7 copy-start.3
  2553.3 3.7 copy-start.19
  2553.3 3.7 copy-start.22
  2553.3 3.7 copy-start.24
  2553.3 3.7 copy-start.26
  2554.9 15.0 copy-start.14
  2557.0 13.0 copy-start.15
  2606.5 4196.9 %all-gather.25.cloned.1.call-start = ((), (), s32[]{:S(2)}) async-start(), calls=%async_computation.12 | async-start | bytes 34560000 | tf_op jit(solution)/shard_map/all_gather | solution.py:176
  2607.1 4656.6 %all-reduce.35.cloned.1.call-start = ((), (), s32[]{:S(2)}) async-start(), calls=%async_computation.14 | async-start | bytes 30736384
  7162.5 27.4 copy-start.27
  7162.5 27.4 copy-start.28
  7162.5 27.4 copy-start.34
  7162.5 27.5 copy-start.1
  7162.5 27.4 copy-start.33
  7207.3 8.5 copy-start.32
  7215.5 44.9 copy-start.10
  7215.5 44.9 copy-start.30
  7215.5 44.9 copy-start.36
Sparse Core Ops, SparseCore 0:
  13.6 42.0 all-gather.18
  58.1 59.2 all-reduce.28
  119.6 39.7 all-gather.22
  161.7 309.5 all-gather.20
  1032.2 28.5 all-gather.12
  1062.8 29.7 all-gather.14
  1097.2 613.4 all-reduce.30
  1712.3 391.6 all-gather.16
  2374.5 60.0 reduce-scatter.2
  2436.9 60.1 reduce-scatter.4
  2606.6 3611.4 all-reduce.32
  6219.5 583.8 all-gather.24
  6806.8 267.0 all-reduce.34
